TPU v7x, 512 devices: a whole 4x8x8 slice. The times are simulated.
512 devices in a mesh: rep: 8 (over z), exp: 64 (over y, x, core).
Axes of the slice: x: 4, y: 8, z: 8, core: 2. Of those that a mesh axis runs over, the one named last changes fastest.
Arguments:
- tokens: bfloat16 [81920, 512], P(('rep', 'exp')), may hold values from -6 to 6
- gates: bfloat16 [81920, 2], P(('rep', 'exp')), may hold values from 0.19921875 to 1
- routes: int32 [81920, 2], P(('rep', 'exp')), may hold values from 0 to 63, all different within a row; in each aligned block of 160 rows (0 to 159, 160 to 319, ...) at most 7 rows name the same one
- cotangent: bfloat16 [81920, 512], P(('rep', 'exp')), may hold values from -6 to 6
- w_up: bfloat16 [64, 2048, 512], P('exp'), may hold values from -0.25 to 0.25
- w_down: bfloat16 [64, 2048, 512], P('exp'), may hold values from -0.125 to 0.125
Outputs:
- d_tokens: bfloat16 [81920, 512], P(('rep', 'exp'))
- d_gates: bfloat16 [81920, 2], P(('rep', 'exp'))
- grad_up: bfloat16 [64, 2048, 512], P('exp', 'rep')
- grad_down: bfloat16 [64, 2048, 512], P('exp', 'rep')
Inputs may be any that keep to these rules, and one draw needn't show every extreme that they name: `routes`: each row names two different experts. In each aligned block of 160 rows (the rows of one device) no expert is named by more than 7 rows, a bound that some block reaches.
All inputs are finite; a program needn't handle non-finite values.
Results may differ from a plain program's by a relative error of at most 0.014.
Values may be sent and summed in bfloat16 or wider, within the bound.
A program may use at most 64 MiB of HBM per device.

v0:
```python
import jax
import jax.numpy as jnp
from jax import lax
from jax.sharding import PartitionSpec as P


def silu_parts(preact):
    sigma = jax.nn.sigmoid(preact)
    return (preact * sigma, sigma * (1.0 + preact * (1.0 - sigma)))


def contract_last(left, right):
    return lax.dot_general(
        left, right, (((1,), (1,)), ((), ())), preferred_element_type=jnp.float32
    )


def contract_first(left, right):
    return lax.dot_general(
        left, right, (((0,), (0,)), ((), ())), preferred_element_type=jnp.float32
    )


def local(tokens, gates, routes, cotangent, w_up, w_down):
    tok_rows = tokens.shape[0]
    feat_dim = tokens.shape[1]
    groups = lax.axis_size("exp")
    mirrors = lax.axis_size("rep")
    capacity = max(2, 3 * tok_rows // groups)
    slots_all = groups * capacity
    flat_ids = routes.reshape(-1)
    onehot = (flat_ids[:, None] == jnp.arange(groups, dtype=jnp.int32)[None, :]).astype(jnp.int32)
    slot_pos = jnp.sum((jnp.cumsum(onehot, axis=0) - 1) * onehot, axis=1)
    target = flat_ids * capacity + slot_pos
    gate_flat = gates.reshape(-1)
    select = (jnp.arange(slots_all, dtype=jnp.int32)[:, None] == target[None, :]).astype(
        jnp.bfloat16
    )
    by_row = select.reshape(slots_all, tok_rows, 2).sum(axis=2)
    rows_out = jnp.dot(by_row, tokens, preferred_element_type=jnp.float32).astype(jnp.bfloat16)
    grads_out = jnp.dot(by_row, cotangent, preferred_element_type=jnp.float32).astype(jnp.bfloat16)
    gate_out = jnp.dot(select, gate_flat, preferred_element_type=jnp.float32).astype(jnp.bfloat16)
    rows_in, grad_in, gate_in = (
        lax.all_to_all(
            rows_out.reshape(groups, capacity, feat_dim),
            "exp",
            split_axis=0,
            concat_axis=0,
            tiled=True,
        ),
        lax.all_to_all(
            grads_out.reshape(groups, capacity, feat_dim),
            "exp",
            split_axis=0,
            concat_axis=0,
            tiled=True,
        ),
        lax.all_to_all(
            gate_out.reshape(groups, capacity), "exp", split_axis=0, concat_axis=0, tiled=True
        ),
    )
    rows_in = rows_in.reshape(slots_all, feat_dim)
    grad_in = grad_in.reshape(slots_all, feat_dim)
    gate_in = gate_in.reshape(slots_all)
    up_mat = w_up[0]
    down_mat = w_down[0]
    preact = contract_last(rows_in, up_mat)
    active, slopes = silu_parts(preact)
    hidden = active.astype(jnp.bfloat16)
    output = jnp.dot(hidden, down_mat, preferred_element_type=jnp.float32)
    gate_grad = jnp.sum(grad_in.astype(jnp.float32) * output, axis=1).astype(jnp.bfloat16)
    out_grad = (gate_in.astype(jnp.float32)[:, None] * grad_in.astype(jnp.float32)).astype(
        jnp.bfloat16
    )
    hid_grad = (contract_last(out_grad, down_mat) * slopes).astype(jnp.bfloat16)
    in_grad = jnp.dot(hid_grad, up_mat, preferred_element_type=jnp.float32).astype(jnp.bfloat16)
    ff_share = up_mat.shape[0] // mirrors
    offset = lax.axis_index("rep") * ff_share
    up_slice = lax.dynamic_slice_in_dim(up_mat, offset, ff_share, 0)
    down_slice = lax.dynamic_slice_in_dim(down_mat, offset, ff_share, 0)

    def one_mirror(mirror_rows, mirror_grads):
        part_pre = contract_last(mirror_rows, up_slice)
        part_act, part_slope = silu_parts(part_pre)
        part_hidden = part_act.astype(jnp.bfloat16)
        part_hid_grad = (contract_last(mirror_grads, down_slice) * part_slope).astype(jnp.bfloat16)
        up_part = contract_first(part_hid_grad, mirror_rows).astype(jnp.bfloat16)
        down_part = contract_first(part_hidden, mirror_grads).astype(jnp.bfloat16)
        return (up_part, down_part)

    piece_rows = lax.all_gather(rows_in, "rep", axis=0, tiled=True)
    piece_grads = lax.all_gather(out_grad, "rep", axis=0, tiled=True)
    shards = piece_rows.shape[0] // slots_all
    stacked_rows = piece_rows.reshape(shards, slots_all, feat_dim)
    stacked_grads = piece_grads.reshape(shards, slots_all, feat_dim)
    up_parts, down_parts = jax.vmap(one_mirror)(stacked_rows, stacked_grads)
    up_sum = jnp.sum(up_parts.astype(jnp.float32), axis=0)
    down_sum = jnp.sum(down_parts.astype(jnp.float32), axis=0)
    grad_up = up_sum.astype(jnp.bfloat16)
    grad_down = down_sum.astype(jnp.bfloat16)
    back_grad, back_gate = (
        lax.all_to_all(
            in_grad.reshape(groups, capacity, feat_dim),
            "exp",
            split_axis=0,
            concat_axis=0,
            tiled=True,
        ),
        lax.all_to_all(
            gate_grad.reshape(groups, capacity), "exp", split_axis=0, concat_axis=0, tiled=True
        ),
    )
    back_grad = back_grad.reshape(slots_all, feat_dim)
    back_gate = back_gate.reshape(slots_all)
    d_tokens = contract_first(by_row, back_grad).astype(jnp.bfloat16)
    d_gates = contract_first(select, back_gate).astype(jnp.bfloat16).reshape(tok_rows, 2)
    return (d_tokens, d_gates, grad_up[None], grad_down[None])


def solution(mesh):
    in_specs = (
        P(("rep", "exp"), None),
        P(("rep", "exp"), None),
        P(("rep", "exp"), None),
        P(("rep", "exp"), None),
        P("exp", None, None),
        P("exp", None, None),
    )
    out_specs = (
        P(("rep", "exp"), None),
        P(("rep", "exp"), None),
        P("exp", "rep", None),
        P("exp", "rep", None),
    )
    return jax.shard_map(local, mesh=mesh, in_specs=in_specs, out_specs=out_specs, check_vma=False)
```

profile of v0, /device:TPU:1, one launch (start us, length us, event | category | flops | bytes accessed | tf_op | source)
XLA Modules:
  0.0 170.5 jit_solution(11793736202481853756)
XLA Ops:
  7.2 0.9 copy.37
  8.4 0.9 reduce-window.6
  9.9 0.7 multiply_add_fusion.1
  10.7 1.2 convolution_convert_fusion
  12.1 29.2 %all_to_all.31 = bf16[64,7,512]{2,1,0:T(8,128)(2,1)} all-to-all(bf16[64,7,512]{2,1,0:T(8,128)(2,1)S(1)} %reshape.116), channel_id=1, replica_groups=mesh['rep'=8,'exp'=64] {'exp'}, dimensions={0} | all-to-all | bytes 917504 | tf_op jit(solution)/shard_map/all_to_all | solution.py:44
  41.3 2.0 %reshape.117 = bf16[448,512]{1,0:T(8,128)(2,1)} reshape(bf16[64,7,512]{2,1,0:T(8,128)(2,1)} %all_to_all.31) | data formatting | bytes 917504 | tf_op jit(solution)/shard_map/reshape | solution.py:62
  43.9 0.8 all_to_all.25
  44.7 5.7 %all-to-all-start = ((bf16[64,1,7]{2,1,0:T(2,128)(2,1)}), bf16[64,1,7]{2,1,0:T(2,128)(2,1)S(1)}, u32[]{:S(2)}, u32[]{:S(2)}) async-start(bf16[64,1,7]{2,1,0:T(2,128)(2,1)} %all_to_all.25), calls=%async_computation | async-start | bytes 65536 | tf_op jit(solution)/shard_map/all_to_all | solution.py:58
  50.7 1.0 reshape.115
  51.7 8.0 %all-to-all-done = bf16[64,1,7]{2,1,0:T(2,128)(2,1)S(1)} async-done(((bf16[64,1,7]{2,1,0:T(2,128)(2,1)}), bf16[64,1,7]{2,1,0:T(2,128)(2,1)S(1)}, u32[]{:S(2)}, u32[]{:S(2)}) %all-to-all-start) | async-done | bytes 928 | tf_op jit(solution)/shard_map/all_to_all | solution.py:58
  59.7 4.7 %all-to-all-start.1 = ((bf16[64,7,512]{2,1,0:T(8,128)(2,1)}), bf16[64,7,512]{2,1,0:T(8,128)(2,1)S(1)}, u32[]{:S(2)}, u32[]{:S(2)}) async-start(bf16[64,7,512]{2,1,0:T(8,128)(2,1)} %reshape.115), calls=%async_computation.1 | async-start | bytes 1048576 | tf_op jit(solution)/shard_map/all_to_all | solution.py:51
  64.7 17.5 %all-to-all-done.1 = bf16[64,7,512]{2,1,0:T(8,128)(2,1)S(1)} async-done(((bf16[64,7,512]{2,1,0:T(8,128)(2,1)}), bf16[64,7,512]{2,1,0:T(8,128)(2,1)S(1)}, u32[]{:S(2)}, u32[]{:S(2)}) %all-to-all-start.1) | async-done | bytes 458784 | tf_op jit(solution)/shard_map/all_to_all | solution.py:51
  82.3 1.1 reshape.126
  83.3 2.1 %multiply_convert_fusion.11 = bf16[448,512]{1,0:T(8,128)(2,1)} fusion(f32[448,512]{1,0:T(8,128)} %reshape.126, f32[448]{0:T(512)S(1)} %reshape.127), kind=kLoop, calls=%fused_computation.24 | loop fusion | flops 458752 | bytes 1378048 | tf_op jit(solution)/shard_map/convert_element_type | solution.py:72
  85.5 1.0 multiply_convert_fusion.10
  86.4 1.2 convert_element_type.103
  87.7 1.1 fusion.2
  88.8 1.9 %copy-done.1 = f32[448,2048]{1,0:T(8,128)} copy-done((f32[448,2048]{1,0:T(8,128)}, f32[448,2048]{1,0:T(8,128)S(1)}, u32[]{:S(2)}) %copy-start.1) | copy-done | bytes 3670040
  90.7 1.2 fusion.14
  92.0 0.8 convert_element_type.124
  92.7 5.7 %all-to-all-start.4 = ((bf16[64,1,7]{2,1,0:T(2,128)(2,1)}), bf16[64,1,7]{2,1,0:T(2,128)(2,1)S(1)}, u32[]{:S(2)}, u32[]{:S(2)}) async-start(bf16[64,1,7]{2,1,0:T(2,128)(2,1)} %convert_element_type.124), calls=%async_computation.4 | async-start | bytes 65536 | tf_op jit(solution)/shard_map/all_to_all | solution.py:109
  98.5 5.1 %fusion.11 = bf16[448,512]{1,0:T(8,128)(2,1)S(1)} fusion(bf16[1,2048,512]{2,1,0:T(8,128)(2,1)S(1)} %copy-done, f32[448,2048]{1,0:T(8,128)} %copy-done.1, bf16[448,512]{1,0:T(8,128)(2,1)S(1)} %convert_element_type.103, bf16[1,2048,512]{2,1,0:T(8,128)(2,1)} %param.11), kind=kOutput, calls=%fused_computation.17 | convolution fusion | flops 1887535104 | bytes 8781824 | tf_op jit(solution)/shard_map/dot_general | solution.py:76
  103.5 0.9 reshape.118
  104.5 3.3 %all-to-all-done.4 = bf16[64,1,7]{2,1,0:T(2,128)(2,1)S(1)} async-done(((bf16[64,1,7]{2,1,0:T(2,128)(2,1)}), bf16[64,1,7]{2,1,0:T(2,128)(2,1)S(1)}, u32[]{:S(2)}, u32[]{:S(2)}) %all-to-all-start.4) | async-done | bytes 928 | tf_op jit(solution)/shard_map/all_to_all | solution.py:109
  107.8 7.0 %all-to-all-start.3 = ((bf16[64,7,512]{2,1,0:T(8,128)(2,1)}), bf16[64,7,512]{2,1,0:T(8,128)(2,1)S(1)}, u32[]{:S(2)}, u32[]{:S(2)}) async-start(bf16[64,7,512]{2,1,0:T(8,128)(2,1)} %reshape.118), calls=%async_computation.3 | async-start | bytes 1048576 | tf_op jit(solution)/shard_map/all_to_all | solution.py:102
  115.4 0.7 copy.44
  116.1 16.4 %all-to-all-done.3 = bf16[64,7,512]{2,1,0:T(8,128)(2,1)S(1)} async-done(((bf16[64,7,512]{2,1,0:T(8,128)(2,1)}), bf16[64,7,512]{2,1,0:T(8,128)(2,1)S(1)}, u32[]{:S(2)}, u32[]{:S(2)}) %all-to-all-start.3) | async-done | bytes 458784 | tf_op jit(solution)/shard_map/all_to_all | solution.py:102
  132.6 0.9 convolution_convert_fusion.2
  133.6 5.1 %fusion.24 = f32[8,448,256]{2,1,0:T(8,128)} fusion(bf16[8,448,512]{2,1,0:T(8,128)(2,1)} %bitcast.60, bf16[1,2048,512]{2,1,0:T(8,128)(2,1)S(1)} %copy-done, s32[]{:T(128)S(6)} %select_n.4), kind=kOutput, calls=%fused_computation.32 | convolution fusion | flops 939524096 | bytes 7602180 | tf_op jit(solution)/shard_map/vmap()/dot_general | solution.py:13
  138.7 10.9 %all-gather.3.cloned.1.call-done = bf16[3584,512]{1,0:T(8,128)(2,1)} async-done(((bf16[448,512]{1,0:T(8,128)(2,1)}), bf16[3584,512]{1,0:T(8,128)(2,1)}) %all-gather.3.cloned.1.call-update) | async-done | bytes 3670032 | tf_op jit(solution)/shard_map/all_gather | solution.py:92
  149.6 8.8 %convert_reduce_fusion.1 = bf16[256,512]{1,0:T(8,128)(2,1)} fusion(bf16[8,448,512]{2,1,0:T(8,128)(2,1)} %bitcast.61, f32[8,448,256]{2,1,0:T(8,128)} %fusion.24, bf16[8,448,512]{2,1,0:T(8,128)(2,1)} %bitcast.65, bf16[1,2048,512]{2,1,0:T(8,128)(2,1)} %param.11, s32[]{:T(128)S(6)} %select_n.4), kind=kOutput, calls=%fused_computation.14 | convolution fusion | flops 1889271808 | bytes 11534340 | tf_op jit(solution)/shard_map/vmap()/dot_general | solution.py:19
  158.4 5.2 %convert_reduce_fusion = bf16[256,512]{1,0:T(8,128)(2,1)} fusion(bf16[8,448,512]{2,1,0:T(8,128)(2,1)} %bitcast.66, f32[8,448,256]{2,1,0:T(8,128)} %fusion.24), kind=kOutput, calls=%fused_computation.13 | convolution fusion | flops 946077696 | bytes 7602176 | tf_op jit(solution)/shard_map/vmap()/dot_general | solution.py:19
  (43 shorter events, 3.1 us)
Async XLA Ops:
  7.2 80.5 %copy-start = (bf16[1,2048,512]{2,1,0:T(8,128)(2,1)S(1)}, bf16[1,2048,512]{2,1,0:T(8,128)(2,1)}, u32[]{:S(2)}) copy-start(bf16[1,2048,512]{2,1,0:T(8,128)(2,1)} %param.10) | copy-start | bytes 6291460
  7.2 36.1 %copy-start.5 = (bf16[160,2]{0,1:T(2,128)(2,1)S(1)}, bf16[160,2]{0,1:T(2,128)(2,1)}, u32[]{:S(2)}) copy-start(bf16[160,2]{0,1:T(2,128)(2,1)} %param.7) | copy-start | bytes 1924
  7.2 43.2 %copy-start.4 = (bf16[160,512]{1,0:T(8,128)(2,1)S(1)}, bf16[160,512]{1,0:T(8,128)(2,1)}, u32[]{:S(2)}) copy-start(bf16[160,512]{1,0:T(8,128)(2,1)} %param.9) | copy-start | bytes 491524
  7.2 126.4 %all-gather.5.cloned.1.call-start = ((), (), s32[]{:S(2)}) async-start(), calls=%async_computation.6 | async-start | bytes 4128768 | tf_op jit(solution)/shard_map/all_gather | solution.py:91
  44.7 15.0 %all-to-all-start = ((bf16[64,1,7]{2,1,0:T(2,128)(2,1)}), bf16[64,1,7]{2,1,0:T(2,128)(2,1)S(1)}, u32[]{:S(2)}, u32[]{:S(2)}) async-start(bf16[64,1,7]{2,1,0:T(2,128)(2,1)} %all_to_all.25), calls=%async_computation | async-start | bytes 65536 | tf_op jit(solution)/shard_map/all_to_all | solution.py:58
  50.7 36.9 %copy-start.2 = (bf16[448,512]{1,0:T(8,128)(2,1)S(1)}, bf16[448,512]{1,0:T(8,128)(2,1)}, u32[]{:S(2)}) copy-start(bf16[448,512]{1,0:T(8,128)(2,1)} %reshape.117) | copy-start | bytes 1376260
  59.7 22.6 %all-to-all-start.1 = ((bf16[64,7,512]{2,1,0:T(8,128)(2,1)}), bf16[64,7,512]{2,1,0:T(8,128)(2,1)S(1)}, u32[]{:S(2)}, u32[]{:S(2)}) async-start(bf16[64,7,512]{2,1,0:T(8,128)(2,1)} %reshape.115), calls=%async_computation.1 | async-start | bytes 1048576 | tf_op jit(solution)/shard_map/all_to_all | solution.py:51
  64.5 85.1 %all-gather.3.cloned.1.call-start = ((), (), s32[]{:S(2)}) async-start(), calls=%async_computation.5 | async-start | bytes 4128768 | tf_op jit(solution)/shard_map/all_gather | solution.py:92
  87.6 3.1 %copy-start.3 = (f32[448,512]{1,0:T(8,128)S(1)}, f32[448,512]{1,0:T(8,128)}, u32[]{:S(2)}) copy-start(f32[448,512]{1,0:T(8,128)} %reshape.126) | copy-start | bytes 2752516
  87.7 3.1 %copy-start.6 = (bf16[1,2048,512]{2,1,0:T(8,128)(2,1)S(1)}, bf16[1,2048,512]{2,1,0:T(8,128)(2,1)}, u32[]{:S(2)}) copy-start(bf16[1,2048,512]{2,1,0:T(8,128)(2,1)} %param.11) | copy-start | bytes 6291460
  88.8 1.9 %copy-start.1 = (f32[448,2048]{1,0:T(8,128)}, f32[448,2048]{1,0:T(8,128)S(1)}, u32[]{:S(2)}) copy-start(f32[448,2048]{1,0:T(8,128)S(1)} %fusion.2) | copy-start | bytes 11010052
  92.7 15.0 %all-to-all-start.4 = ((bf16[64,1,7]{2,1,0:T(2,128)(2,1)}), bf16[64,1,7]{2,1,0:T(2,128)(2,1)S(1)}, u32[]{:S(2)}, u32[]{:S(2)}) async-start(bf16[64,1,7]{2,1,0:T(2,128)(2,1)} %convert_element_type.124), calls=%async_computation.4 | async-start | bytes 65536 | tf_op jit(solution)/shard_map/all_to_all | solution.py:109
  107.8 24.7 %all-to-all-start.3 = ((bf16[64,7,512]{2,1,0:T(8,128)(2,1)}), bf16[64,7,512]{2,1,0:T(8,128)(2,1)S(1)}, u32[]{:S(2)}, u32[]{:S(2)}) async-start(bf16[64,7,512]{2,1,0:T(8,128)(2,1)} %reshape.118), calls=%async_computation.3 | async-start | bytes 1048576 | tf_op jit(solution)/shard_map/all_to_all | solution.py:102
Sparse Core Ops, SparseCore 0:
  43.4 52.6 all-gather.4
  98.2 51.3 all-gather.2
where the time goes:
time: 171 us; the launch traced here: 170 us
  waiting for transfers between devices  56.2 us (33%)
  matrix products  29.6 us (17%)
  blocking collectives  29.2 us (17%)
  starting transfers between devices  23.2 us (14%)
  between operations  14.3 us (8%)
  local copies, waits for them, and re-layouts  12.8 us (7%)
  other arithmetic  5.21 us (3%)
    all_to_all x1, blocking collectives, local(): lax.all_to_all(rows_out.reshape(groups, capacity, feat_dim), 'exp', split...  29.2 us
    all_to_all x1, waiting for transfers between devices, local(): lax.all_to_all(grads_out.reshape(groups, capacity, feat_dim), 'exp', spli...  17.5 us
    all_to_all x1, waiting for transfers between devices, local(): lax.all_to_all(in_grad.reshape(groups, capacity, feat_dim), 'exp', split_...  16.4 us
    dot_general x4, matrix products, contract_first(): lax.dot_general(left, right, (((0,), (0,)), ((), ())), preferred_element_...  15.2 us
    all_gather x1, waiting for transfers between devices, local(): piece_grads = lax.all_gather(out_grad, 'rep', axis=0, tiled=True)  10.9 us
    all_to_all x1, waiting for transfers between devices, local(): lax.all_to_all(gate_out.reshape(groups, capacity), 'exp', split_axis=0, c...  8.03 us
    all_to_all x1, starting transfers between devices, local(): lax.all_to_all(in_grad.reshape(groups, capacity, feat_dim), 'exp', split_...  6.99 us
    dot_general x2, matrix products, contract_last(): lax.dot_general(left, right, (((1,), (1,)), ((), ())), preferred_element_...  6.27 us
  transfers between devices with their start and end apart: 6, of which 5 were waited for; matrix products, arithmetic and copies ran while one was open for 14% of the time, Pallas kernels for 0%

commit v1 on v0

v1 whole, which is shorter than its diff:
```python
import functools
import jax
import jax.numpy as jnp
from jax import lax
from jax.experimental import pallas as pl
from jax.experimental.pallas import tpu as pltpu
from jax.sharding import PartitionSpec as P

MESH = pl.DeviceIdType.MESH
F32, BF16, I32 = jnp.float32, jnp.bfloat16, jnp.int32
SLOT = 8
Y, X, C = 8, 4, 2
PARTS = 2


def mm(a, b):
    return lax.dot_general(a, b, (((1,), (0,)), ((), ())), preferred_element_type=F32)


def mm_nt(a, b):
    return lax.dot_general(a, b, (((1,), (1,)), ((), ())), preferred_element_type=F32)


def mm_tn(a, b):
    return lax.dot_general(a, b, (((0,), (0,)), ((), ())), preferred_element_type=F32)


def iota(shape, dim):
    return lax.broadcasted_iota(I32, shape, dim)


def peer_of(me, k):
    a = k % Y
    dy = lax.rem(Y + ((a + 1) // 2) * (2 * (a % 2) - 1), Y)
    b = k // Y
    y = lax.rem(me // (X * C) + dy, Y)
    x = lax.rem((me // C) % X + b // C, X)
    c = lax.rem(me % C + b % C, C)
    return (y * X + x) * C + c


def kernel(
    tok_ref, gate_ref, route_ref, cot_ref, wu_hbm, wd_hbm,
    dtok_ref, dgate_ref, gup_ref, gdn_ref,
    wu, wd, snd, rcv, xs, gs, hid, hgr, acc, dg, bsnd, brcv,
    usnd, dsnd, urcv, drcv,
    wsem, ssem, rsem, bssem, brsem, us, ur, ds, dr,
):
    z = lax.axis_index("rep")
    me = lax.axis_index("exp")
    nz = usnd.shape[0] + 1
    n = snd.shape[0]
    tok_rows, feat = tok_ref.shape
    slots = n * SLOT
    ff = wu.shape[0] // nz
    part = ff // PARTS
    nxt, prv = lax.rem(z + 1, nz), lax.rem(z + nz - 1, nz)

    barrier = pltpu.get_barrier_semaphore()

    @pl.loop(1, n)
    def _(k):
        pl.semaphore_signal(barrier, inc=1, device_id=(z, peer_of(me, k)), device_id_type=MESH)

    pl.semaphore_signal(barrier, inc=1, device_id=(nxt, me), device_id_type=MESH)
    pl.semaphore_signal(barrier, inc=1, device_id=(prv, me), device_id_type=MESH)
    wcopies = [
        pltpu.make_async_copy(wu_hbm.at[0], wu, wsem.at[0]),
        pltpu.make_async_copy(wd_hbm.at[0], wd, wsem.at[1]),
    ]
    for copy in wcopies:
        copy.start()

    routes = route_ref[...]
    gates = gate_ref[...].astype(F32)
    cot = cot_ref[...].astype(F32)
    expert = iota((tok_rows, n), 1)
    hot = [routes[:, k : k + 1] == expert for k in range(2)]
    both = jnp.logical_or(hot[0], hot[1]).astype(F32).astype(BF16)
    row_i, col_i = iota((tok_rows, tok_rows), 0), iota((tok_rows, tok_rows), 1)
    before = mm((row_i > col_i).astype(F32).astype(BF16), both)
    pos = [jnp.sum(jnp.where(h, before, 0.0), axis=1, keepdims=True) for h in hot]
    target = [routes[:, k : k + 1].astype(F32) * SLOT + pos[k] for k in range(2)]
    slot_i = iota((slots, tok_rows), 0).astype(F32)
    sel = []
    for k in range(2):
        as_row = jnp.sum(jnp.where(row_i == col_i, target[k], 0.0), axis=0, keepdims=True)
        sel.append((slot_i == as_row).astype(F32))
    rows = mm((sel[0] + sel[1]).astype(BF16), tok_ref[...])
    grads = mm(sel[0].astype(BF16), (gates[:, 0:1] * cot).astype(BF16))
    grads += mm(sel[1].astype(BF16), (gates[:, 1:2] * cot).astype(BF16))
    snd[:, 0] = rows.reshape(n, SLOT, feat).astype(BF16)
    snd[:, 1] = grads.reshape(n, SLOT, feat).astype(BF16)
    rcv[me] = snd[me]

    pl.semaphore_wait(barrier, n + 1)

    @pl.loop(1, n)
    def _(k):
        peer = peer_of(me, k)
        pltpu.make_async_remote_copy(
            src_ref=snd.at[peer], dst_ref=rcv.at[me], send_sem=ssem, recv_sem=rsem,
            device_id=(z, peer), device_id_type=MESH,
        ).start()

    acc[...] = jnp.zeros_like(acc)
    dg[...] = jnp.zeros_like(dg)
    for copy in wcopies:
        copy.wait()
    others = pl.ds(0, n - 1)
    pltpu.make_async_copy(rcv.at[others], rcv.at[others], rsem).wait()
    xs[...] = rcv[:, 0].astype(F32).reshape(slots, feat).astype(BF16)
    gs[...] = rcv[:, 1].astype(F32).reshape(slots, feat).astype(BF16)

    def expert_part(order):
        half = order // 2 + 1
        off = (2 * (order % 2) - 1) * half + (order // (nz - 1)) * (nz // 2)
        at = pl.ds(pl.multiple_of(lax.rem(z + nz + off, nz) * ff, ff), ff)
        up, down = wu[at, :], wd[at, :]
        pre = mm_nt(up, xs[...])
        back = mm_nt(down, gs[...])
        sigma = jax.nn.sigmoid(pre)
        hidden = (pre * sigma).astype(BF16)
        slope = sigma * (1.0 + pre * (1.0 - sigma))
        grad = (back * slope).astype(BF16)
        hid[at, :] = hidden
        hgr[at, :] = grad
        dg[...] += jnp.sum((hidden.astype(F32) * back).reshape(ff // 8, 8, slots), axis=0)
        acc[...] += mm_tn(grad, up)

    def ring(step, c, up):
        snd_buf, rcv_buf, s_sem, r_sem = (usnd, urcv, us, ur) if up else (dsnd, drcv, ds, dr)
        at = pl.ds(c * part, part)
        return pltpu.make_async_remote_copy(
            src_ref=snd_buf.at[step, at], dst_ref=rcv_buf.at[step, at],
            send_sem=s_sem.at[step, c], recv_sem=r_sem.at[step, c],
            device_id=(nxt if up else prv, me), device_id_type=MESH,
        )

    def partial(shard, c, up):
        at = pl.ds(pl.multiple_of(shard * ff + c * part, part), part)
        return mm(hgr[at, :], xs[...]) if up else mm(hid[at, :], gs[...])

    def ring_step(step, first):
        for c in range(PARTS):
            for up in (True, False):
                shard = lax.rem(z + nz - 1 - step, nz) if up else lax.rem(z + 1 + step, nz)
                value = partial(shard, c, up)
                at = pl.ds(c * part, part)
                if not first:
                    ring(step - 1, c, up).wait_recv()
                    value += (urcv if up else drcv)[step - 1, at].astype(F32)
                (usnd if up else dsnd)[step, at] = value.astype(BF16)
                ring(step, c, up).start()

    def two_parts(step):
        @pl.loop(0, 2)
        def _(k):
            expert_part(2 * step + k)

    two_parts(0)
    ring_step(0, True)

    @pl.loop(1, nz // 2)
    def _(step):
        two_parts(step)
        ring_step(step, False)

    gate_row = jnp.sum(dg[...], axis=0, keepdims=True)
    gi, si = iota((n, slots), 0), iota((n, slots), 1)
    spread = jnp.where(si // SLOT == gi, gate_row, 0.0).astype(BF16)
    lane = iota((slots, feat), 1)
    place = (iota((slots, feat), 0) % SLOT == lane).astype(F32).astype(BF16)
    gate_out = mm(spread, place)
    packed = acc[...].reshape(n, SLOT, feat)
    packed = jnp.where(iota((n, SLOT, feat), 1) == SLOT - 1, gate_out[:, None, :], packed)
    bsnd[...] = packed.astype(BF16)
    brcv[me] = bsnd[me]

    @pl.loop(1, n)
    def _(k):
        peer = peer_of(me, k)
        pltpu.make_async_remote_copy(
            src_ref=bsnd.at[peer], dst_ref=brcv.at[me], send_sem=bssem, recv_sem=brsem,
            device_id=(z, peer), device_id_type=MESH,
        ).start()

    @pl.loop(nz // 2, nz - 1)
    def _(step):
        ring_step(step, False)

    pltpu.make_async_copy(brcv.at[others], brcv.at[others], brsem).wait()
    slot_l = iota((tok_rows, slots), 1).astype(F32)
    owned = jnp.logical_or(slot_l == target[0], slot_l == target[1]).astype(F32).astype(BF16)
    returned = brcv[...].astype(F32).reshape(slots, feat).astype(BF16)
    dtok_ref[...] = mm(owned, returned).astype(BF16)
    gate_back = brcv[:, SLOT - 1, 0:128]
    lane_i = iota((tok_rows, 128), 1).astype(F32)
    gates_out = []
    for k in range(2):
        rows_k = mm(hot[k].astype(F32).astype(BF16), gate_back)
        value = jnp.sum(jnp.where(lane_i == pos[k], rows_k, 0.0), axis=1, keepdims=True)
        gates_out.append(value / gates[:, k : k + 1])
    col = iota((tok_rows, 2), 1)
    dgate_ref[...] = jnp.where(col == 0, gates_out[0], gates_out[1]).astype(BF16)

    last = nz - 2
    for c in range(PARTS):
        at = pl.ds(c * part, part)
        for up in (True, False):
            value = partial(z, c, up)
            ring(last, c, up).wait_recv()
            value += (urcv if up else drcv)[last, at].astype(F32)
            (gup_ref if up else gdn_ref)[0, at] = value.astype(BF16)

    pltpu.make_async_copy(snd.at[others], snd.at[others], ssem).wait()
    pltpu.make_async_copy(bsnd.at[others], bsnd.at[others], bssem).wait()

    @pl.loop(0, nz - 1)
    def _(step):
        for c in range(PARTS):
            for up in (True, False):
                ring(step, c, up).wait_send()


def local(tokens, gates, routes, cotangent, w_up, w_down):
    tok_rows, feat = tokens.shape
    n = lax.axis_size("exp")
    nz = lax.axis_size("rep")
    hidden = w_up.shape[1]
    ff = hidden // nz
    slots = n * SLOT
    vmem = pl.BlockSpec(memory_space=pltpu.VMEM)
    hbm = pl.BlockSpec(memory_space=pl.ANY)
    V = pltpu.VMEM
    dma = pltpu.SemaphoreType.DMA
    return pl.pallas_call(
        kernel,
        out_shape=(
            jax.ShapeDtypeStruct((tok_rows, feat), BF16),
            jax.ShapeDtypeStruct((tok_rows, 2), BF16),
            jax.ShapeDtypeStruct((1, ff, feat), BF16),
            jax.ShapeDtypeStruct((1, ff, feat), BF16),
        ),
        in_specs=[vmem, vmem, vmem, vmem, hbm, hbm],
        out_specs=(vmem, vmem, vmem, vmem),
        scratch_shapes=[
            V((hidden, feat), BF16), V((hidden, feat), BF16),
            V((n, 2, SLOT, feat), BF16), V((n, 2, SLOT, feat), BF16),
            V((slots, feat), BF16), V((slots, feat), BF16),
            V((hidden, slots), BF16), V((hidden, slots), BF16),
            V((slots, feat), F32), V((8, slots), F32),
            V((n, SLOT, feat), BF16), V((n, SLOT, feat), BF16),
        ]
        + [V((nz - 1, ff, feat), BF16)] * 4
        + [dma((2,)), dma, dma, dma, dma]
        + [dma((nz - 1, PARTS))] * 4,
        compiler_params=pltpu.CompilerParams(
            collective_id=0, has_side_effects=True, vmem_limit_bytes=60 * 2**20
        ),
        name="expert_backward",
    )(tokens, gates, routes, cotangent, w_up, w_down)


def solution(mesh):
    in_specs = (
        P(("rep", "exp"), None),
        P(("rep", "exp"), None),
        P(("rep", "exp"), None),
        P(("rep", "exp"), None),
        P("exp", None, None),
        P("exp", None, None),
    )
    out_specs = (
        P(("rep", "exp"), None),
        P(("rep", "exp"), None),
        P("exp", "rep", None),
        P("exp", "rep", None),
    )
    return jax.shard_map(local, mesh=mesh, in_specs=in_specs, out_specs=out_specs, check_vma=False)
```

time: 171 us -> 99.1 us (0.58)
  Pallas kernels: 0 us -> 88.9 us
  waiting for transfers between devices: 56.2 us -> 0 us
  matrix products: 29.6 us -> 0 us
  blocking collectives: 29.2 us -> 0 us
  starting transfers between devices: 23.2 us -> 0 us
  between operations: 14.3 us -> 0.64 us
  other arithmetic: 5.21 us -> 0 us
  local copies, waits for them, and re-layouts: 12.8 us -> 9.21 us
    pallas_call x0 -> x1, Pallas kernels: none -> 88.9 us  [local(): pl.pallas_call(kernel, out_shape=(jax.ShapeDtypeStruct((tok_rows, feat),...]
    all_to_all x4 -> x0, waiting for transfers between devices: 45.2 us -> none  [the longest x1 17.5 us: local(): lax.all_to_all(grads_out.reshape(groups, capacity, feat_dim), 'exp', spli...]
    dot_general x11 -> x0, matrix products: 29.6 us -> none  [the longest x4 15.2 us: contract_first(): lax.dot_general(left, right, (((0,), (0,)), ((), ())), preferred_element_...]
    all_to_all x1 -> x0, blocking collectives: 29.2 us -> none  [local(): lax.all_to_all(rows_out.reshape(groups, capacity, feat_dim), 'exp', split...]
    all_to_all x4 -> x0, starting transfers between devices: 23.1 us -> none  [the longest x1 6.99 us: local(): lax.all_to_all(in_grad.reshape(groups, capacity, feat_dim), 'exp', split_...]
    all_gather x2 -> x0, waiting for transfers between devices: 10.9 us -> none  [the longest x1 10.9 us: local(): piece_grads = lax.all_gather(out_grad, 'rep', axis=0, tiled=True)]
    reshape x8 -> x0, local copies, waits for them, and re-layouts: 4.63 us -> none  [the longest x1 1.96 us: local(): rows_in = rows_in.reshape(slots_all, feat_dim)]
    unnamed x17 -> x5, local copies, waits for them, and re-layouts: 3.66 us -> 7.78 us
  transfers between devices with their start and end apart: 6 -> 0, of which waited for: 5 -> 0; matrix products, arithmetic and copies ran while one was open for 14% -> 0% of each run, Pallas kernels for 0% -> 0%
where the time goes in v1:
time: 99.1 us; the launch traced here: 98.7 us
  Pallas kernels  88.9 us (90%)
  local copies, waits for them, and re-layouts  9.21 us (9%)
    pallas_call x1, Pallas kernels, local(): pl.pallas_call(kernel, out_shape=(jax.ShapeDtypeStruct((tok_rows, feat),...  88.9 us
    unnamed x5, local copies, waits for them, and re-layouts  7.78 us

profile of v1, /device:TPU:1, one launch (start us, length us, event | category | flops | bytes accessed | tf_op | source)
XLA Modules:
  0.0 98.7 jit_solution(7498931213406319640)
XLA Ops:
  0.6 1.4 %copy.10.gate_ref = bf16[160,2]{1,0:T(8,128)(2,1)} copy(bf16[160,2]{0,1:T(2,128)(2,1)} %param.7) | data formatting | bytes 1280 | tf_op args[1]
  2.0 1.4 %copy.11.route_ref = s32[160,2]{1,0:T(8,128)} copy(s32[160,2]{0,1:T(2,128)} %param.8) | data formatting | bytes 2560 | tf_op args[2]
  3.5 88.9 %expert_backward.1 = (bf16[160,512]{1,0:T(8,128)(2,1)}, bf16[160,2]{1,0:T(8,128)(2,1)}, bf16[1,256,512]{2,1,0:T(8,128)(2,1)}, bf16[1,256,512]{2,1,0:T(8,128)(2,1)}) custom-call(bf16[160,512]{1,0:T(8,128)(2,1)} %tok_ref.1, bf16[160,2]{1,0:T(8,128)(2,1)} %copy.10.gate_ref, s32[160,2]{1,0:T(8,128)} %copy.11.route_ref, bf16[160,512]{1,0:T(8,128)(2,1)} %cot_ref.1, ...), custom_call_target="tpu_custom_call" | custom-call | tf_op jit(solution)/shard_map/expert_backward/pallas_call | solution.py:237
  92.4 1.4 %copy.12 = bf16[160,2]{0,1:T(2,128)(2,1)} copy(bf16[160,2]{1,0:T(8,128)(2,1)} %get-tuple-element.5) | data formatting | bytes 1280 | tf_op jit(solution)/shard_map/expert_backward/pallas_call | solution.py:237
  93.8 1.6 %copy.16 = bf16[160,512]{1,0:T(8,128)(2,1)} copy(bf16[160,512]{1,0:T(8,128)(2,1)} %get-tuple-element.12) | data formatting | bytes 327680
  95.4 1.7 %copy.17 = bf16[1,256,512]{2,1,0:T(8,128)(2,1)} copy(bf16[1,256,512]{2,1,0:T(8,128)(2,1)} %get-tuple-element.14) | data formatting | bytes 524288
  97.1 1.7 %copy.18 = bf16[1,256,512]{2,1,0:T(8,128)(2,1)} copy(bf16[1,256,512]{2,1,0:T(8,128)(2,1)} %get-tuple-element.15) | data formatting | bytes 524288

commit v2 on v1

v2 whole, which is shorter than its diff:
```python
import functools
import jax
import jax.numpy as jnp
from jax import lax
from jax.experimental import pallas as pl
from jax.experimental.pallas import tpu as pltpu
from jax.sharding import PartitionSpec as P

MESH = pl.DeviceIdType.MESH
F32, BF16, I32 = jnp.float32, jnp.bfloat16, jnp.int32
CAP, SLOT, LANE = 7, 8, 128
Y, X, C = 8, 4, 2
ROW = X * C
PARTS = 2
LONG, SHORT = 3, 2


def mm(a, b):
    return lax.dot_general(a, b, (((1,), (0,)), ((), ())), preferred_element_type=F32)


def mm_nt(a, b):
    return lax.dot_general(a, b, (((1,), (1,)), ((), ())), preferred_element_type=F32)


def mm_tn(a, b):
    return lax.dot_general(a, b, (((0,), (0,)), ((), ())), preferred_element_type=F32)


def iota(shape, dim):
    return lax.broadcasted_iota(I32, shape, dim)


def mask16(m):
    return m.astype(F32).astype(BF16)


def kernel(
    tok_ref, gate_ref, route_ref, cot_ref, wu_hbm, wd_hbm,
    dtok_ref, dgate_ref, gup_ref, gdn_ref,
    wu, wd, snd, rcv, nb, pack, tmp, x3, g3, x2, g2, th, tg, acc, dg, ret, bsnd, brcv,
    ring_s, ring_r, base,
    wsem, lsem, ssem, rsem, fs, fr, bssem, brsem, rs, rr,
):
    z = lax.axis_index("rep")
    me = lax.axis_index("exp")
    nz = lax.axis_size("rep")
    n = snd.shape[0]
    tok_rows, feat = tok_ref.shape
    chunks = feat // LANE
    slots = n * SLOT
    ff = wu.shape[0] // nz
    part = ff // PARTS
    nxt, prv = lax.rem(z + 1, nz), lax.rem(z + nz - 1, nz)
    my_y, my_x, my_c = me // ROW, lax.rem(me // C, X), lax.rem(me, C)
    offs = [lax.rem(my_x + b // C, X) * C + lax.rem(my_c + b % C, C) for b in range(ROW)]

    def row_at(a):
        half = (a + 1) // 2
        return lax.rem(my_y + Y + (2 * lax.rem(a, 2) - 1) * half, Y)

    def each_peer(visit):
        for b in range(1, ROW):
            visit(my_y * ROW + offs[b])

        @pl.loop(1, Y)
        def _(a):
            first = row_at(a) * ROW
            for b in range(ROW):
                visit(first + offs[b])

    barrier = pltpu.get_barrier_semaphore()
    each_peer(
        lambda peer: pl.semaphore_signal(
            barrier, inc=1, device_id=(z, peer), device_id_type=MESH
        )
    )
    pl.semaphore_signal(barrier, inc=1, device_id=(nxt, me), device_id_type=MESH)
    pl.semaphore_signal(barrier, inc=1, device_id=(prv, me), device_id_type=MESH)
    wcopies = [
        pltpu.make_async_copy(wu_hbm.at[0], wu, wsem.at[0]),
        pltpu.make_async_copy(wd_hbm.at[0], wd, wsem.at[1]),
    ]
    for copy in wcopies:
        copy.start()

    routes = route_ref[...]
    gates = gate_ref[...].astype(F32)
    row_i, col_i = iota((tok_rows, tok_rows), 0), iota((tok_rows, tok_rows), 1)
    eye = row_i == col_i

    def column(v):
        return jnp.sum(jnp.where(eye, v, 0.0), axis=1, keepdims=True)

    expert = iota((n, tok_rows), 0)
    ids = [routes[k : k + 1, :] for k in range(2)]
    hot = [ids[k] == expert for k in range(2)]
    before = mm(mask16(jnp.logical_or(hot[0], hot[1])), mask16(row_i < col_i))
    pos = [jnp.sum(jnp.where(h, before, 0.0), axis=0, keepdims=True) for h in hot]
    slot_i = iota((n * CAP, tok_rows), 0).astype(F32)
    sel = [(slot_i == pos[k] * n + ids[k].astype(F32)).astype(F32) for k in range(2)]
    cot = cot_ref[...].astype(F32)
    rows = mm((sel[0] + sel[1]).astype(BF16), tok_ref[...])
    grads = mm(sel[0].astype(BF16), (column(gates[0:1, :]) * cot).astype(BF16))
    grads += mm(sel[1].astype(BF16), (column(gates[1:2, :]) * cot).astype(BF16))
    for s in range(CAP):
        for r in range(chunks):
            at = slice(r * LANE, (r + 1) * LANE)
            pack[s, pl.ds(r, n, stride=SLOT), :] = rows[s * n : (s + 1) * n, at]
            pack[s, pl.ds(chunks + r, n, stride=SLOT), :] = grads[s * n : (s + 1) * n, at]
    for s in range(CAP):
        snd[:, :, s * LANE : (s + 1) * LANE] = pack[s].reshape(n, SLOT, LANE).astype(BF16)

    pl.semaphore_wait(barrier, n + 1)
    own = pltpu.make_async_copy(snd.at[me], rcv.at[me], lsem)
    own.start()
    each_peer(
        lambda peer: pltpu.make_async_remote_copy(
            src_ref=snd.at[peer], dst_ref=rcv.at[me], send_sem=ssem, recv_sem=rsem.at[my_y],
            device_id=(z, peer), device_id_type=MESH,
        ).start()
    )

    x3[:, ROW * CAP :] = jnp.zeros_like(x3[:, ROW * CAP :])
    g3[:, ROW * CAP :] = jnp.zeros_like(g3[:, ROW * CAP :])
    acc[...] = jnp.zeros_like(acc)
    dg[...] = jnp.zeros_like(dg)

    def forward(side, g):
        at = pl.ds(g * ROW, ROW)
        return pltpu.make_async_remote_copy(
            src_ref=rcv.at[at], dst_ref=nb.at[side, at], send_sem=fs, recv_sem=fr.at[side, g],
            device_id=((nxt, prv)[side], me), device_id_type=MESH,
        )

    def unpack(block, m, g):
        for s in range(CAP):
            tile = block[:, :, s * LANE : (s + 1) * LANE].astype(F32)
            tmp[s] = tile.reshape(ROW * SLOT, LANE)
        for s in range(CAP):
            for r in range(chunks):
                at = slice(r * LANE, (r + 1) * LANE)
                x3[m, s * Y + g, :, at] = tmp[s, pl.ds(r, ROW, stride=SLOT), :].astype(BF16)
                g3[m, s * Y + g, :, at] = tmp[s, pl.ds(chunks + r, ROW, stride=SLOT), :].astype(BF16)

    def arrived(a, count):
        g = row_at(a)
        got = rcv.at[pl.ds(0, count)]
        pltpu.make_async_copy(got, got, rsem.at[g]).wait()
        forward(0, g).start()
        forward(1, g).start()
        unpack(rcv[pl.ds(g * ROW, ROW)], 1, g)

    def flat(m):
        x2[m] = x3[m].astype(F32).reshape(slots, feat).astype(BF16)
        g2[m] = g3[m].astype(F32).reshape(slots, feat).astype(BF16)

    def neighbours(a):
        g = row_at(a)
        for side in range(2):
            forward(side, g).wait_recv()
            unpack(nb[side, pl.ds(g * ROW, ROW)], 2 * side, g)

    own.wait()
    arrived(0, ROW - 1)

    @pl.loop(1, Y)
    def _(a):
        arrived(a, ROW)

    for copy in wcopies:
        copy.wait()
    flat(1)

    def front(m, shard):
        at = pl.ds(pl.multiple_of(shard * ff, ff), ff)
        up = wu[at, :]
        pre = mm_nt(up, x2[m])
        back = mm_nt(wd[at, :], g2[m])
        sigma = jax.nn.sigmoid(pre)
        hidden = (pre * sigma).astype(BF16)
        grad = (back * (sigma * (1.0 + pre * (1.0 - sigma)))).astype(BF16)
        return up, hidden, grad, back

    def own_part(shard, save):
        up, hidden, grad, back = front(1, shard)
        if save:
            th[2 * LONG + 2] = hidden
            tg[2 * LONG + 2] = grad
        dg[...] += jnp.sum((hidden.astype(F32) * back).reshape(ff // 8, 8, slots), axis=0)
        acc[...] += mm_tn(grad, up)

    def side_parts(j):
        for side in (1, 0):
            shard = lax.rem(z + nz - LONG + j, nz) if side else lax.rem(z + LONG - j, nz)
            _, hidden, grad, _ = front(2 * side, shard)
            th[(LONG + 1) * side + j] = hidden
            tg[(LONG + 1) * side + j] = grad

    own_part(z, True)

    @pl.loop(0, Y - 2)
    def _(a):
        neighbours(a)

    own_part(lax.rem(z + 1, nz), False)

    @pl.loop(Y - 2, Y)
    def _(a):
        neighbours(a)

    flat(2)
    flat(0)

    def product(is_up, m, idx, at):
        return mm(tg[idx, at], x2[m]) if is_up else mm(th[idx, at], g2[m])

    def hop(side, slot, c):
        at = pl.ds(c * part, part)
        return pltpu.make_async_remote_copy(
            src_ref=ring_s.at[side, slot, at], dst_ref=ring_r.at[side, slot, at],
            send_sem=rs.at[side, slot, c], recv_sem=rr.at[side, slot, c],
            device_id=((nxt, prv)[side], me), device_id_type=MESH,
        )

    def send(is_long, j):
        slot = j if is_long else SHORT + j
        first = j == 0 if is_long else j == 1
        for c in range(PARTS):
            at = pl.ds(c * part, part)
            for side in (1, 0):
                value = product(is_long == (side == 1), 2 * side, (LONG + 1) * side + j, at)
                if not first:
                    hop(side, slot - 1, c).wait_recv()
                    value += ring_r[side, slot - 1, at].astype(F32)
                ring_s[side, slot, at] = value.astype(BF16)
                hop(side, slot, c).start()

    side_parts(0)
    send(True, 0)
    side_parts(1)
    send(False, 1)

    @pl.loop(2, nz)
    def _(i):
        own_part(lax.rem(z + i, nz), False)

    gate_row = jnp.sum(dg[...], axis=0, keepdims=True)
    spread = jnp.where(iota((n, slots), 1) % n == iota((n, slots), 0), gate_row, 0.0)
    place = mask16(iota((slots, LANE), 0) // n == iota((slots, LANE), 1))
    gate_out = mm(spread.astype(BF16), place)
    for r in range(chunks):
        at = slice(r * LANE, (r + 1) * LANE)
        for s in range(CAP):
            ret[r, pl.ds(s, n, stride=SLOT), :] = acc[s * n : (s + 1) * n, at]
        ret[r, pl.ds(CAP, n, stride=SLOT), :] = gate_out
    for r in range(chunks):
        bsnd[:, :, r * LANE : (r + 1) * LANE] = ret[r].reshape(n, SLOT, LANE).astype(BF16)
    own_back = pltpu.make_async_copy(bsnd.at[me], brcv.at[me], lsem)
    own_back.start()
    each_peer(
        lambda peer: pltpu.make_async_remote_copy(
            src_ref=bsnd.at[peer], dst_ref=brcv.at[me], send_sem=bssem, recv_sem=brsem,
            device_id=(z, peer), device_id_type=MESH,
        ).start()
    )

    send(True, 1)
    side_parts(2)
    send(False, 2)
    send(True, 2)
    side_parts(3)
    everything = pl.ds(0, ff)
    mine = ((0, LONG), (1, 2 * LONG + 2), (2, 2 * LONG + 1))
    for which in range(2):
        base[which] = sum(product(which == 0, m, idx, everything) for m, idx in mine)

    own_back.wait()
    others = pl.ds(0, n - 1)
    pltpu.make_async_copy(brcv.at[others], brcv.at[others], brsem).wait()
    slot_l = iota((tok_rows, slots), 1).astype(F32)
    places = [column(ids[k].astype(F32) * SLOT + pos[k]) for k in range(2)]
    owned = mask16(jnp.logical_or(slot_l == places[0], slot_l == places[1]))
    returned = brcv[...].astype(F32).reshape(slots, feat).astype(BF16)
    dtok_ref[...] = mm(owned, returned).astype(BF16)
    gate_back = brcv[:, CAP, 0:LANE]
    which_slot = iota((LANE, tok_rows), 0).astype(F32)
    gates_out = []
    for k in range(2):
        mixed = mm_tn(gate_back, mask16(hot[k]))
        value = jnp.sum(jnp.where(which_slot == pos[k], mixed, 0.0), axis=0, keepdims=True)
        gates_out.append(value / gates[k : k + 1, :])
    first_row = iota((2, tok_rows), 0) == 0
    dgate_ref[...] = jnp.where(first_row, gates_out[0], gates_out[1]).astype(BF16)

    for c in range(PARTS):
        at = pl.ds(c * part, part)
        for side in (1, 0):
            hop(side, LONG + SHORT - 1, c).wait_recv()
            base[side, at] += ring_r[side, LONG + SHORT - 1, at].astype(F32)
        for side in (1, 0):
            hop(side, LONG - 1, c).wait_recv()
            value = base[1 - side, at] + ring_r[side, LONG - 1, at].astype(F32)
            (gup_ref if side else gdn_ref)[0, at] = value.astype(BF16)

    pltpu.make_async_copy(snd.at[others], snd.at[others], ssem).wait()
    pltpu.make_async_copy(bsnd.at[others], bsnd.at[others], bssem).wait()
    pltpu.make_async_copy(nb, nb, fs).wait()
    for side in range(2):
        for slot in range(LONG + SHORT):
            for c in range(PARTS):
                hop(side, slot, c).wait_send()


def finish(*refs):
    for src, dst in zip(refs[:4], refs[4:]):
        dst[...] = src[...]


def local(tokens, gates, routes, cotangent, w_up, w_down):
    tok_rows, feat = tokens.shape
    n = lax.axis_size("exp")
    nz = lax.axis_size("rep")
    hidden = w_up.shape[1]
    ff = hidden // nz
    slots = n * SLOT
    vmem = pl.BlockSpec(memory_space=pltpu.VMEM)
    hbm = pl.BlockSpec(memory_space=pl.ANY)
    V = pltpu.VMEM
    dma = pltpu.SemaphoreType.DMA
    hops = LONG + SHORT
    tiles = 2 * LONG + 3
    shapes = (
        jax.ShapeDtypeStruct((tok_rows, feat), BF16),
        jax.ShapeDtypeStruct((2, tok_rows), BF16),
        jax.ShapeDtypeStruct((1, ff, feat), BF16),
        jax.ShapeDtypeStruct((1, ff, feat), BF16),
    )
    outs = pl.pallas_call(
        kernel,
        out_shape=shapes,
        in_specs=[vmem, vmem, vmem, vmem, hbm, hbm],
        out_specs=(vmem, vmem, vmem, vmem),
        scratch_shapes=[
            V((hidden, feat), BF16), V((hidden, feat), BF16),
            V((n, SLOT, CAP * LANE), BF16), V((n, SLOT, CAP * LANE), BF16),
            V((2, n, SLOT, CAP * LANE), BF16),
            V((CAP, n * SLOT, LANE), F32), V((CAP, ROW * SLOT, LANE), F32),
            V((3, n, SLOT, feat), BF16), V((3, n, SLOT, feat), BF16),
            V((3, slots, feat), BF16), V((3, slots, feat), BF16),
            V((tiles, ff, slots), BF16), V((tiles, ff, slots), BF16),
            V((slots, feat), F32), V((8, slots), F32),
            V((feat // LANE, slots, LANE), F32),
            V((n, SLOT, feat), BF16), V((n, SLOT, feat), BF16),
            V((2, hops, ff, feat), BF16), V((2, hops, ff, feat), BF16),
            V((2, ff, feat), F32),
            dma((2,)), dma, dma, dma((Y,)), dma, dma((2, Y)), dma, dma,
            dma((2, hops, PARTS)), dma((2, hops, PARTS)),
        ],
        compiler_params=pltpu.CompilerParams(
            collective_id=0, has_side_effects=True, vmem_limit_bytes=60 * 2**20
        ),
        name="expert_backward",
    )(tokens, gates.T, routes.T, cotangent, w_up, w_down)
    d_tokens, d_gates, grad_up, grad_down = pl.pallas_call(
        finish,
        out_shape=shapes,
        in_specs=[vmem] * 4,
        out_specs=(vmem,) * 4,
        compiler_params=pltpu.CompilerParams(vmem_limit_bytes=4 * 2**20),
        name="finish",
    )(*outs)
    return d_tokens, d_gates.T, grad_up, grad_down


def solution(mesh):
    in_specs = (
        P(("rep", "exp"), None),
        P(("rep", "exp"), None),
        P(("rep", "exp"), None),
        P(("rep", "exp"), None),
        P("exp", None, None),
        P("exp", None, None),
    )
    out_specs = (
        P(("rep", "exp"), None),
        P(("rep", "exp"), None),
        P("exp", "rep", None),
        P("exp", "rep", None),
    )
    return jax.shard_map(local, mesh=mesh, in_specs=in_specs, out_specs=out_specs, check_vma=False)
```

time: 99.1 us -> 85.1 us (0.86)
  Pallas kernels: 88.9 us -> 80.8 us
  local copies, waits for them, and re-layouts: 9.21 us -> 3.47 us
    pallas_call x1 -> x2, Pallas kernels: 88.9 us -> 80.8 us  [the longest x1 79.9 us: local(): pl.pallas_call(kernel, out_shape=shapes, in_specs=[vmem, vmem, vmem, vmem...]
    unnamed x5 -> x8, local copies, waits for them, and re-layouts: 7.78 us -> 3.47 us
    pallas_call x1 -> x0, local copies, waits for them, and re-layouts: 1.43 us -> none  [local(): pl.pallas_call(kernel, out_shape=(jax.ShapeDtypeStruct((tok_rows, feat),...]
where the time goes in v2:
time: 85.1 us; the launch traced here: 84.9 us
  Pallas kernels  80.8 us (95%)
  local copies, waits for them, and re-layouts  3.47 us (4%)
    pallas_call x1, Pallas kernels, local(): pl.pallas_call(kernel, out_shape=shapes, in_specs=[vmem, vmem, vmem, vmem...  79.9 us
    unnamed x8, local copies, waits for them, and re-layouts  3.47 us

profile of v2, /device:TPU:1, one launch (start us, length us, event | category | flops | bytes accessed | tf_op | source)
XLA Modules:
  0.0 84.9 jit_solution(8080913551678085033)
XLA Ops:
  0.6 79.9 %expert_backward.1 = (bf16[160,512]{1,0:T(8,128)(2,1)}, bf16[2,160]{1,0:T(2,128)(2,1)}, bf16[1,256,512]{2,1,0:T(8,128)(2,1)}, bf16[1,256,512]{2,1,0:T(8,128)(2,1)}) custom-call(bf16[160,512]{1,0:T(8,128)(2,1)} %tok_ref.1, bf16[2,160]{1,0:T(2,128)(2,1)} %bitcast.4, s32[2,160]{1,0:T(2,128)} %bitcast.3, bf16[160,512]{1,0:T(8,128)(2,1)} %cot_ref.1, ...), custom_call_target="tpu_custom_call" | custom-call | tf_op jit(solution)/shard_map/expert_backward/pallas_call | solution.py:339
  80.5 0.0 copy-start
  80.5 0.9 %copy-done = bf16[1,256,512]{2,1,0:T(8,128)(2,1)S(1)} copy-done((bf16[1,256,512]{2,1,0:T(8,128)(2,1)S(1)}, bf16[1,256,512]{2,1,0:T(8,128)(2,1)}, u32[]{:S(2)}) %copy-start) | copy-done | bytes 262168
  81.5 0.0 copy-start.1
  81.5 0.9 %copy-done.1 = bf16[1,256,512]{2,1,0:T(8,128)(2,1)S(1)} copy-done((bf16[1,256,512]{2,1,0:T(8,128)(2,1)S(1)}, bf16[1,256,512]{2,1,0:T(8,128)(2,1)}, u32[]{:S(2)}) %copy-start.1) | copy-done | bytes 262168
  82.4 0.0 copy-start.2
  82.4 0.9 %copy-done.2 = bf16[160,512]{1,0:T(8,128)(2,1)S(1)} copy-done((bf16[160,512]{1,0:T(8,128)(2,1)S(1)}, bf16[160,512]{1,0:T(8,128)(2,1)}, u32[]{:S(2)}) %copy-start.2) | copy-done | bytes 163864
  83.3 0.0 copy-start.3
  83.3 0.7 copy-done.3
  84.0 0.9 %finish.1 = (bf16[160,512]{1,0:T(8,128)(2,1)}, bf16[2,160]{1,0:T(2,128)(2,1)}, bf16[1,256,512]{2,1,0:T(8,128)(2,1)}, bf16[1,256,512]{2,1,0:T(8,128)(2,1)}) custom-call(bf16[160,512]{1,0:T(8,128)(2,1)S(1)} %copy-done.2, bf16[2,160]{1,0:T(2,128)(2,1)S(1)} %copy-done.3, bf16[1,256,512]{2,1,0:T(8,128)(2,1)S(1)} %copy-done, bf16[1,256,512]{2,1,0:T(8,128)(2,1)S(1)} %copy-done.1), custom_call_target="tpu_custom_call" | custom-call | tf_op jit(solution)/shard_map/finish/pallas_call | solution.py:365
Async XLA Ops:
  80.5 1.0 %copy-start = (bf16[1,256,512]{2,1,0:T(8,128)(2,1)S(1)}, bf16[1,256,512]{2,1,0:T(8,128)(2,1)}, u32[]{:S(2)}) copy-start(bf16[1,256,512]{2,1,0:T(8,128)(2,1)} %get-tuple-element.14.refs_2_) | copy-start | bytes 786436
  81.5 0.9 %copy-start.1 = (bf16[1,256,512]{2,1,0:T(8,128)(2,1)S(1)}, bf16[1,256,512]{2,1,0:T(8,128)(2,1)}, u32[]{:S(2)}) copy-start(bf16[1,256,512]{2,1,0:T(8,128)(2,1)} %get-tuple-element.15.refs_3_) | copy-start | bytes 786436
  82.4 0.9 %copy-start.2 = (bf16[160,512]{1,0:T(8,128)(2,1)S(1)}, bf16[160,512]{1,0:T(8,128)(2,1)}, u32[]{:S(2)}) copy-start(bf16[160,512]{1,0:T(8,128)(2,1)} %get-tuple-element.12.refs_0_) | copy-start | bytes 491524
  83.3 0.7 copy-start.3
